TPU v7x, 128 devices: a whole 4x4x4 slice. The times are simulated.
128 devices in a mesh: samp: 32 (over x, y, core), var: 4 (over z).
Axes of the slice: x: 4, y: 4, z: 4, core: 2. Of those that a mesh axis runs over, the one named last changes fastest.
Arguments:
- genotypes: int32 [32768, 4096], P('samp', 'var'), may hold values from 0 to 2
- observed: int32 [32768, 4096], P('samp', 'var'), may hold values from 0 to 1, as said below
- proportions: float32 [10, 32768], P(None, 'samp'), may hold values from 0 to 1, as said below
- frequencies: float32 [10, 4096], P(None, ('samp', 'var')), may hold values from 0.02 to 0.98
Outputs:
- mixture: float32 [10, 32768], P(None, 'samp')
- alleles: float32 [10, 4096], P(None, 'var')
Inputs may be any that keep to these rules, and one draw needn't show every extreme that they name: Every sample is observed at 256 or more variants and every variant at 2048 or more samples. Each sample's 10 proportions are positive and sum to one.
All inputs are finite; a program needn't handle non-finite values.
Results may differ from a plain program's by a relative error of at most 0.0003.
Values sent between devices are 32-bit elements; how exact they have to be, the bound alone decides.
A program may use at most 128 MiB of HBM per device.

v0:
```python
import jax
import jax.numpy as jnp
from jax import lax
from jax.sharding import PartitionSpec as P

STEPS = 2
CLIP_LOW = 1e-05
NORM_EPS = 1e-10
EXACT = lax.Precision.HIGHEST


def clip_unit(values):
    return jnp.clip(values, CLIP_LOW, 1.0 - CLIP_LOW)


def tidy_mixture(mixture):
    clipped = clip_unit(mixture)
    return clipped / jnp.sum(clipped, axis=0, keepdims=True)


def step_size(first, second):
    return jnp.maximum(1.0, jnp.sqrt(first / (second + NORM_EPS)))


def allele_rule(alleles, alt_sums, ref_sums):
    weighted = alleles * alt_sums
    return clip_unit(weighted / (weighted + (1.0 - alleles) * ref_sums))


def local(genotypes, observed, proportions, frequencies):
    var_count = lax.axis_size("var")
    gathered = lax.all_gather(frequencies, ("samp", "var"), axis=1, tiled=True)
    owner_width = gathered.shape[1] // var_count
    alleles = lax.dynamic_slice_in_dim(
        gathered, lax.axis_index("var") * owner_width, owner_width, 1
    )
    seen_vals = observed.astype(jnp.float32)
    geno_vals = genotypes.astype(jnp.float32)
    alt_counts = seen_vals * geno_vals
    ref_counts = seen_vals * (2.0 - geno_vals)
    local_counts = jnp.sum(observed, axis=1).astype(jnp.float32)
    twice_observed = 2.0 * lax.psum(local_counts, "var")[None, :]

    def expectation_step(mixture, current):
        expected = lax.dot_general(
            mixture,
            current,
            (((0,), (0,)), ((), ())),
            precision=EXACT,
            preferred_element_type=jnp.float32,
        )
        ratio_alt = alt_counts / expected
        ratio_ref = ref_counts / (1.0 - expected)
        prop_terms = lax.dot_general(
            current,
            ratio_alt - ratio_ref,
            (((1,), (1,)), ((), ())),
            precision=EXACT,
            preferred_element_type=jnp.float32,
        )
        prop_terms = prop_terms + jnp.sum(ratio_ref, axis=1)[None, :]
        alt_terms = lax.dot_general(
            mixture,
            ratio_alt,
            (((1,), (0,)), ((), ())),
            precision=EXACT,
            preferred_element_type=jnp.float32,
        )
        ref_terms = lax.dot_general(
            mixture,
            ratio_ref,
            (((1,), (0,)), ((), ())),
            precision=EXACT,
            preferred_element_type=jnp.float32,
        )
        prop_sums = lax.psum(prop_terms, "var")
        next_mixture = clip_unit(mixture * prop_sums / twice_observed)
        alt_sums, ref_sums = lax.psum((alt_terms, ref_terms), "samp")
        next_alleles = allele_rule(current, alt_sums, ref_sums)
        return (next_mixture, next_alleles)

    mixture = proportions
    for repeat in range(STEPS):
        mixture_one, alleles_one = expectation_step(mixture, alleles)
        mixture_two, alleles_two = expectation_step(mixture_one, alleles_one)
        step_mix = mixture_one - mixture
        curve_mix = mixture_two - mixture_one - step_mix
        step_allele = alleles_one - alleles
        curve_allele = alleles_two - alleles_one - step_allele
        step_mix_local = jnp.sum(step_mix * step_mix)
        curve_mix_local = jnp.sum(curve_mix * curve_mix)
        step_allele_local = jnp.sum(step_allele * step_allele)
        curve_allele_local = jnp.sum(curve_allele * curve_allele)
        step_allele_sum, curve_allele_sum = lax.psum((step_allele_local, curve_allele_local), "var")
        step_mix_sum, curve_mix_sum = lax.psum((step_mix_local, curve_mix_local), "samp")
        alpha_mix = step_size(step_mix_sum, curve_mix_sum)
        alpha_allele = step_size(step_allele_sum, curve_allele_sum)
        extra_mix = tidy_mixture(
            mixture + 2.0 * alpha_mix * step_mix + alpha_mix * alpha_mix * curve_mix
        )
        extra_allele = clip_unit(
            alleles + 2.0 * alpha_allele * step_allele + alpha_allele * alpha_allele * curve_allele
        )
        mixture, alleles = expectation_step(extra_mix, extra_allele)
    return (mixture, alleles)


def solution(mesh):
    placed = (P("samp", "var"), P("samp", "var"), P(None, "samp"), P(None, ("samp", "var")))
    return jax.shard_map(
        local,
        mesh=mesh,
        in_specs=placed,
        out_specs=(P(None, "samp"), P(None, "var")),
        check_vma=False,
    )
```

profile of v0, /device:TPU:1, one launch (start us, length us, event | category | flops | bytes accessed | tf_op | source)
XLA Modules:
  0.0 985.0 jit_solution(3233084332891088129)
XLA Ops:
  7.2 64.1 %all-gather = f32[128,32,10]{1,2,0:T(8,128)S(1)} all-gather(f32[1,32,10]{1,2,0:T(8,128)} %bitcast.70), channel_id=1, replica_groups=mesh['samp'=32,'var'=4] {'samp','var'}, dimensions={0}, use_global_device_ids=true | all-gather | bytes 165120 | tf_op jit(solution)/shard_map/all_gather | solution.py:32
  71.8 5.4 copy.14
  77.2 5.4 copy.13
  82.6 12.0 %fusion.78 = (f32[1024]{0:T(1024)S(1)}, f32[1024,1024]{0,1:T(8,128)S(1)}, f32[1024,1024]{0,1:T(8,128)}, f32[1024,1024]{0,1:T(8,128)S(1)}, f32[1024,1024]{1,0:T(8,128)S(1)}) fusion(s32[1024,1024]{0,1:T(8,128)} %copy.14, s32[1024,1024]{0,1:T(8,128)} %copy.13, f32[10,1024]{1,0:T(8,128)S(1)} %copy-done.11, f32[4096,10]{0,1:T(8,128)S(1)} %reshape.15, ...), kind=kOutput, calls=%fused_computation.104 | convolution fusion | flops 134216704 | bytes 25300996 | tf_op jit(solution)/shard_map/dot_general | solution.py:45
  96.5 4.3 convolution_bitcast_fusion
  100.8 4.7 convolution_bitcast_fusion.1
  105.5 10.7 %all-reduce.20.cloned.1.call-start = ((), (), s32[]{:S(2)}) async-start(), calls=%async_computation.2 | async-start | bytes 262144 | tf_op jit(solution)/shard_map/psum | solution.py:78
  118.6 7.4 fusion.13
  126.0 13.1 %all-reduce.8 = (f32[10,1024]{1,0:T(8,128)S(1)}, f32[1024]{0:T(1024)S(1)}) all-reduce(f32[10,1024]{1,0:T(8,128)S(1)} %fusion.13, f32[1024]{0:T(1024)S(1)} %convert_element_type.11), channel_id=1, replica_groups=mesh['samp'=32,'var'=4] {'var'}, use_global_device_ids=true, to_apply=%region_1.0 | all-reduce | flops 11264 | bytes 90112 | tf_op jit(solution)/shard_map/psum | solution.py:76
  139.2 65.9 %all-reduce.22.cloned.1.call-done = (f32[10,1024]{1,0:T(8,128)}, f32[10,1024]{1,0:T(8,128)}) async-done(((f32[10,1024]{1,0:T(8,128)}, f32[10,1024]{1,0:T(8,128)}), (f32[10,1024]{1,0:T(8,128)}, f32[10,1024]{1,0:T(8,128)})) %all-reduce.22.cloned.1.call-update) | async-done | bytes 81936 | tf_op jit(solution)/shard_map/psum | solution.py:78
  206.6 9.0 fusion.77
  225.4 14.0 %psum.194 = f32[10,1024]{1,0:T(8,128)S(1)} all-reduce(f32[10,1024]{1,0:T(8,128)S(1)} %fusion.16), channel_id=1, replica_groups=mesh['samp'=32,'var'=4] {'var'}, use_global_device_ids=true, to_apply=%region_9.10 | all-reduce | flops 10240 | bytes 81920 | tf_op jit(solution)/shard_map/psum | solution.py:76
  240.0 125.1 %all-reduce.23 = (f32[10,1024]{1,0:T(8,128)S(1)}, f32[10,1024]{1,0:T(8,128)S(1)}, f32[]{:T(128)}, f32[]{:T(128)}) all-reduce(f32[10,1024]{1,0:T(8,128)S(1)} %fusion.80, f32[10,1024]{1,0:T(8,128)S(1)} %fusion.65, f32[]{:T(128)} %get-tuple-element.5, f32[]{:T(128)} %get-tuple-element.4), channel_id=1, replica_groups=mesh['samp'=32,'var'=4] {'samp'}, use_global_device_ids=true, to_apply=%region_16.17 | all-reduce | flops 20482 | bytes 163856 | tf_op jit(solution)/shard_map/psum | solution.py:78
  367.0 7.0 all-reduce.7
  375.5 9.0 fusion.73
  388.7 4.2 fusion.49
  392.9 7.3 fusion.19
  400.3 12.7 %psum.200 = f32[10,1024]{1,0:T(8,128)S(1)} all-reduce(f32[10,1024]{1,0:T(8,128)S(1)} %fusion.19), channel_id=1, replica_groups=mesh['samp'=32,'var'=4] {'var'}, use_global_device_ids=true, to_apply=%region_20.21 | all-reduce | flops 10240 | bytes 81920 | tf_op jit(solution)/shard_map/psum | solution.py:76
  413.3 106.5 %all-reduce.20.cloned.1.call-done = (f32[10,1024]{1,0:T(8,128)}, f32[10,1024]{1,0:T(8,128)}) async-done(((f32[10,1024]{1,0:T(8,128)}, f32[10,1024]{1,0:T(8,128)}), (f32[10,1024]{1,0:T(8,128)}, f32[10,1024]{1,0:T(8,128)})) %all-reduce.20.cloned.1.call-update) | async-done | bytes 81936 | tf_op jit(solution)/shard_map/psum | solution.py:78
  520.7 9.0 fusion.72
  533.9 4.2 fusion.81
  538.1 7.3 fusion.22
  545.4 13.9 %psum.203 = f32[10,1024]{1,0:T(8,128)S(1)} all-reduce(f32[10,1024]{1,0:T(8,128)S(1)} %fusion.22), channel_id=1, replica_groups=mesh['samp'=32,'var'=4] {'var'}, use_global_device_ids=true, to_apply=%region_24.25 | all-reduce | flops 10240 | bytes 81920 | tf_op jit(solution)/shard_map/psum | solution.py:76
  559.7 102.3 %all-reduce.18.cloned.1.call-done = (f32[10,1024]{1,0:T(8,128)}, f32[10,1024]{1,0:T(8,128)}) async-done(((f32[10,1024]{1,0:T(8,128)}, f32[10,1024]{1,0:T(8,128)}), (f32[10,1024]{1,0:T(8,128)}, f32[10,1024]{1,0:T(8,128)})) %all-reduce.18.cloned.1.call-update) | async-done | bytes 81936 | tf_op jit(solution)/shard_map/psum | solution.py:78
  663.0 9.0 fusion.71
  681.7 13.9 %psum.207 = f32[10,1024]{1,0:T(8,128)S(1)} all-reduce(f32[10,1024]{1,0:T(8,128)S(1)} %fusion.25), channel_id=1, replica_groups=mesh['samp'=32,'var'=4] {'var'}, use_global_device_ids=true, to_apply=%region_30.31 | all-reduce | flops 10240 | bytes 81920 | tf_op jit(solution)/shard_map/psum | solution.py:76
  696.3 125.1 %all-reduce.24 = (f32[10,1024]{1,0:T(8,128)S(1)}, f32[10,1024]{1,0:T(8,128)S(1)}, f32[]{:T(128)}, f32[]{:T(128)}) all-reduce(f32[10,1024]{1,0:T(8,128)S(1)} %fusion.82, f32[10,1024]{1,0:T(8,128)S(1)} %fusion.57, f32[]{:T(128)} %get-tuple-element.3, f32[]{:T(128)} %get-tuple-element.2), channel_id=1, replica_groups=mesh['samp'=32,'var'=4] {'samp'}, use_global_device_ids=true, to_apply=%region_37.38 | all-reduce | flops 20482 | bytes 163856 | tf_op jit(solution)/shard_map/psum | solution.py:78
  824.0 6.9 all-reduce.6
  832.3 9.0 fusion.68
  849.8 7.3 fusion.28
  857.1 12.7 %psum.213 = f32[10,1024]{1,0:T(8,128)S(1)} all-reduce(f32[10,1024]{1,0:T(8,128)S(1)} %fusion.28), channel_id=1, replica_groups=mesh['samp'=32,'var'=4] {'var'}, use_global_device_ids=true, to_apply=%region_41.42 | all-reduce | flops 10240 | bytes 81920 | tf_op jit(solution)/shard_map/psum | solution.py:76
  870.5 106.0 %all-reduce.16.cloned.1.call-done = (f32[10,1024]{1,0:T(8,128)}, f32[10,1024]{1,0:T(8,128)}) async-done(((f32[10,1024]{1,0:T(8,128)}, f32[10,1024]{1,0:T(8,128)}), (f32[10,1024]{1,0:T(8,128)}, f32[10,1024]{1,0:T(8,128)})) %all-reduce.16.cloned.1.call-update) | async-done | bytes 81936 | tf_op jit(solution)/shard_map/psum | solution.py:78
  (68 shorter events, 50.7 us)
Async XLA Ops:
  7.2 197.9 %all-reduce.22.cloned.1.call-start = ((), (), s32[]{:S(2)}) async-start(), calls=%async_computation.3 | async-start | bytes 262144 | tf_op jit(solution)/shard_map/psum | solution.py:78
  77.2 5.4 copy-start.11
  94.6 2.0 copy-start
  94.6 6.2 copy-start.4
  94.6 6.2 copy-start.10
  105.5 414.3 %all-reduce.20.cloned.1.call-start = ((), (), s32[]{:S(2)}) async-start(), calls=%async_computation.2 | async-start | bytes 262144 | tf_op jit(solution)/shard_map/psum | solution.py:78
  206.6 9.0 copy-start.5
  375.5 9.1 copy-start.6
  384.5 4.2 copy-start.13
  384.5 4.2 copy-start.2
  413.0 249.0 %all-reduce.18.cloned.1.call-start = ((), (), s32[]{:S(2)}) async-start(), calls=%async_computation.1 | async-start | bytes 262144 | tf_op jit(solution)/shard_map/psum | solution.py:78
  520.7 9.1 copy-start.7
  529.7 4.2 copy-start.14
  529.7 4.2 copy-start.3
  559.4 417.1 %all-reduce.16.cloned.1.call-start = ((), (), s32[]{:S(2)}) async-start(), calls=%async_computation | async-start | bytes 262144 | tf_op jit(solution)/shard_map/psum | solution.py:78
  663.0 9.0 copy-start.8
  832.3 9.1 copy-start.9
  841.4 4.2 copy-start.12
  841.4 4.2 copy-start.1
Sparse Core Ops, SparseCore 0:
  105.6 99.4 all-reduce.21
  413.2 106.5 all-reduce.19
  559.5 102.4 all-reduce.17
  870.0 106.4 all-reduce.15
where the time goes:
time: 994 us; the launch traced here: 985 us
  blocking collectives  409 us (41%)
  waiting for transfers between devices  381 us (38%)
  matrix products  140 us (14%)
  between operations  19.9 us (2%)
  local copies, waits for them, and re-layouts  13.3 us (1%)
  other arithmetic  11.3 us (1%)
  starting transfers between devices  11.2 us (1%)
    psum x4, waiting for transfers between devices, expectation_step(): alt_sums, ref_sums = lax.psum((alt_terms, ref_terms), 'samp')  381 us
    psum x2, blocking collectives, expectation_step(): alt_sums, ref_sums = lax.psum((alt_terms, ref_terms), 'samp')  250 us
    psum x6, blocking collectives, expectation_step(): prop_sums = lax.psum(prop_terms, 'var')  80.4 us
    all_gather x1, blocking collectives, local(): gathered = lax.all_gather(frequencies, ('samp', 'var'), axis=1, tiled=True)  64.1 us
    dot_general x6, matrix products, expectation_step(): lax.dot_general(mixture, current, (((0,), (0,)), ((), ())), precision=EXA...  57.1 us
    dot_general x6, matrix products, expectation_step(): lax.dot_general(current, ratio_alt - ratio_ref, (((1,), (1,)), ((), ())),...  34.7 us
    dot_general x6, matrix products, expectation_step(): lax.dot_general(mixture, ratio_alt, (((1,), (0,)), ((), ())), precision=E...  24.2 us
    dot_general x6, matrix products, expectation_step(): lax.dot_general(mixture, ratio_ref, (((1,), (0,)), ((), ())), precision=E...  24 us
  transfers between devices with their start and end apart: 4, of which 4 were waited for; matrix products, arithmetic and copies ran while one was open for 1% of the time, Pallas kernels for 0%

commit v1 on v0

--- a/solution.py
+++ b/solution.py
@@ -73,7 +73,7 @@
             precision=EXACT,
             preferred_element_type=jnp.float32,
         )
-        prop_sums = lax.psum(prop_terms, "var")
+        prop_sums = lax.all_gather(prop_terms, "var").sum(axis=0)
         next_mixture = clip_unit(mixture * prop_sums / twice_observed)
         alt_sums, ref_sums = lax.psum((alt_terms, ref_terms), "samp")
         next_alleles = allele_rule(current, alt_sums, ref_sums)

time: 994 us -> 978 us (0.984)
  blocking collectives: 409 us -> 399 us
    psum x6 -> x1, blocking collectives: 80.4 us -> 7.43 us  [local(): twice_observed = 2.0 * lax.psum(local_counts, 'var')[None, :]]
    all_gather x0 -> x6, blocking collectives: none -> 59.6 us  [expectation_step(): prop_sums = lax.all_gather(prop_terms, 'var').sum(axis=0)]
where the time goes in v1:
time: 978 us; the launch traced here: 969 us
  blocking collectives  399 us (41%)
  waiting for transfers between devices  375 us (38%)
  matrix products  140 us (14%)
  between operations  19.8 us (2%)
  local copies, waits for them, and re-layouts  13.3 us (1%)
  other arithmetic  11.5 us (1%)
  starting transfers between devices  11 us (1%)
    psum x4, waiting for transfers between devices, expectation_step(): alt_sums, ref_sums = lax.psum((alt_terms, ref_terms), 'samp')  374 us
    psum x2, blocking collectives, expectation_step(): alt_sums, ref_sums = lax.psum((alt_terms, ref_terms), 'samp')  249 us
    all_gather x1, blocking collectives, local(): gathered = lax.all_gather(frequencies, ('samp', 'var'), axis=1, tiled=True)  64.1 us
    all_gather x6, blocking collectives, expectation_step(): prop_sums = lax.all_gather(prop_terms, 'var').sum(axis=0)  59.6 us
    dot_general x6, matrix products, expectation_step(): lax.dot_general(mixture, current, (((0,), (0,)), ((), ())), precision=EXA...  57.1 us
    dot_general x6, matrix products, expectation_step(): lax.dot_general(current, ratio_alt - ratio_ref, (((1,), (1,)), ((), ())),...  34.7 us
    dot_general x6, matrix products, expectation_step(): lax.dot_general(mixture, ratio_alt, (((1,), (0,)), ((), ())), precision=E...  24.2 us
    dot_general x6, matrix products, expectation_step(): lax.dot_general(mixture, ratio_ref, (((1,), (0,)), ((), ())), precision=E...  24 us
  transfers between devices with their start and end apart: 4, of which 4 were waited for; matrix products, arithmetic and copies ran while one was open for 1% of the time, Pallas kernels for 0%

profile of v1, /device:TPU:1, one launch (start us, length us, event | category | flops | bytes accessed | tf_op | source)
XLA Modules:
  0.0 968.6 jit_solution(5159945845993591590)
XLA Ops:
  7.2 64.1 %all-gather.6 = f32[128,32,10]{1,2,0:T(8,128)S(1)} all-gather(f32[1,32,10]{1,2,0:T(8,128)} %bitcast.82), channel_id=1, replica_groups=mesh['samp'=32,'var'=4] {'samp','var'}, dimensions={0}, use_global_device_ids=true | all-gather | bytes 165120 | tf_op jit(solution)/shard_map/all_gather | solution.py:32
  71.8 5.4 copy.14
  77.2 5.4 copy.13
  82.6 12.0 %fusion.96 = (f32[1024]{0:T(1024)S(1)}, f32[1024,1024]{0,1:T(8,128)S(1)}, f32[1024,1024]{0,1:T(8,128)}, f32[1024,1024]{0,1:T(8,128)S(1)}, f32[1024,1024]{1,0:T(8,128)S(1)}) fusion(s32[1024,1024]{0,1:T(8,128)} %copy.14, s32[1024,1024]{0,1:T(8,128)} %copy.13, f32[10,1024]{1,0:T(8,128)S(1)} %copy-done.11, f32[4096,10]{0,1:T(8,128)S(1)} %reshape.21, ...), kind=kOutput, calls=%fused_computation.110 | convolution fusion | flops 134216704 | bytes 25300996 | tf_op jit(solution)/shard_map/dot_general | solution.py:45
  96.5 4.3 convolution_bitcast_fusion
  100.8 4.7 convolution_bitcast_fusion.1
  105.5 10.5 %all-reduce.19.cloned.1.call-start = ((), (), s32[]{:S(2)}) async-start(), calls=%async_computation.2 | async-start | bytes 262144 | tf_op jit(solution)/shard_map/psum | solution.py:78
  118.5 7.4 psum.147
  125.9 7.3 fusion.16
  133.3 9.8 %all-gather.7 = f32[4,10,1024]{2,1,0:T(8,128)S(1)} all-gather(f32[1,10,1024]{2,1,0:T(8,128)S(1)} %fusion.16), channel_id=2, replica_groups=mesh['samp'=32,'var'=4] {'var'}, dimensions={0}, use_global_device_ids=true | all-gather | bytes 204800 | tf_op jit(solution)/shard_map/all_gather | solution.py:76
  143.1 62.0 %all-reduce.21.cloned.1.call-done = (f32[10,1024]{1,0:T(8,128)}, f32[10,1024]{1,0:T(8,128)}) async-done(((f32[10,1024]{1,0:T(8,128)}, f32[10,1024]{1,0:T(8,128)}), (f32[10,1024]{1,0:T(8,128)}, f32[10,1024]{1,0:T(8,128)})) %all-reduce.21.cloned.1.call-update) | async-done | bytes 81936 | tf_op jit(solution)/shard_map/psum | solution.py:78
  206.6 9.0 fusion.95
  225.4 10.4 %all-gather.8 = f32[4,10,1024]{2,1,0:T(8,128)S(1)} all-gather(f32[1,10,1024]{2,1,0:T(8,128)S(1)} %fusion.22), channel_id=3, replica_groups=mesh['samp'=32,'var'=4] {'var'}, dimensions={0}, use_global_device_ids=true | all-gather | bytes 204800 | tf_op jit(solution)/shard_map/all_gather | solution.py:76
  236.4 124.6 %all-reduce.22 = (f32[10,1024]{1,0:T(8,128)S(1)}, f32[10,1024]{1,0:T(8,128)S(1)}, f32[]{:T(128)}, f32[]{:T(128)}) all-reduce(f32[10,1024]{1,0:T(8,128)S(1)} %fusion.98, f32[10,1024]{1,0:T(8,128)S(1)} %fusion.83, f32[]{:T(128)} %get-tuple-element.5, f32[]{:T(128)} %get-tuple-element.4), channel_id=1, replica_groups=mesh['samp'=32,'var'=4] {'samp'}, use_global_device_ids=true, to_apply=%region_16.17 | all-reduce | flops 20482 | bytes 163856 | tf_op jit(solution)/shard_map/psum | solution.py:78
  362.9 9.2 all-reduce.7
  373.6 9.0 fusion.91
  391.0 7.3 fusion.28
  398.4 9.4 all-gather.9
  408.0 105.5 %all-reduce.19.cloned.1.call-done = (f32[10,1024]{1,0:T(8,128)}, f32[10,1024]{1,0:T(8,128)}) async-done(((f32[10,1024]{1,0:T(8,128)}, f32[10,1024]{1,0:T(8,128)}), (f32[10,1024]{1,0:T(8,128)}, f32[10,1024]{1,0:T(8,128)})) %all-reduce.19.cloned.1.call-update) | async-done | bytes 81936 | tf_op jit(solution)/shard_map/psum | solution.py:78
  514.4 9.0 fusion.90
  527.7 4.2 fusion.99
  531.9 7.3 fusion.34
  539.2 10.4 %all-gather.10 = f32[4,10,1024]{2,1,0:T(8,128)S(1)} all-gather(f32[1,10,1024]{2,1,0:T(8,128)S(1)} %fusion.34), channel_id=5, replica_groups=mesh['samp'=32,'var'=4] {'var'}, dimensions={0}, use_global_device_ids=true | all-gather | bytes 204800 | tf_op jit(solution)/shard_map/all_gather | solution.py:76
  549.9 101.9 %all-reduce.17.cloned.1.call-done = (f32[10,1024]{1,0:T(8,128)}, f32[10,1024]{1,0:T(8,128)}) async-done(((f32[10,1024]{1,0:T(8,128)}, f32[10,1024]{1,0:T(8,128)}), (f32[10,1024]{1,0:T(8,128)}, f32[10,1024]{1,0:T(8,128)})) %all-reduce.17.cloned.1.call-update) | async-done | bytes 81936 | tf_op jit(solution)/shard_map/psum | solution.py:78
  652.7 9.0 fusion.89
  671.5 10.4 %all-gather.11 = f32[4,10,1024]{2,1,0:T(8,128)S(1)} all-gather(f32[1,10,1024]{2,1,0:T(8,128)S(1)} %fusion.40), channel_id=6, replica_groups=mesh['samp'=32,'var'=4] {'var'}, dimensions={0}, use_global_device_ids=true | all-gather | bytes 204800 | tf_op jit(solution)/shard_map/all_gather | solution.py:76
  682.5 124.6 %all-reduce.23 = (f32[10,1024]{1,0:T(8,128)S(1)}, f32[10,1024]{1,0:T(8,128)S(1)}, f32[]{:T(128)}, f32[]{:T(128)}) all-reduce(f32[10,1024]{1,0:T(8,128)S(1)} %fusion.100, f32[10,1024]{1,0:T(8,128)S(1)} %fusion.75, f32[]{:T(128)} %get-tuple-element.3, f32[]{:T(128)} %get-tuple-element.2), channel_id=1, replica_groups=mesh['samp'=32,'var'=4] {'samp'}, use_global_device_ids=true, to_apply=%region_37.38 | all-reduce | flops 20482 | bytes 163856 | tf_op jit(solution)/shard_map/psum | solution.py:78
  809.7 9.0 all-reduce.6
  820.2 9.0 fusion.86
  837.6 7.3 fusion.46
  844.9 9.4 all-gather.12
  855.0 105.1 %all-reduce.15.cloned.1.call-done = (f32[10,1024]{1,0:T(8,128)}, f32[10,1024]{1,0:T(8,128)}) async-done(((f32[10,1024]{1,0:T(8,128)}, f32[10,1024]{1,0:T(8,128)}), (f32[10,1024]{1,0:T(8,128)}, f32[10,1024]{1,0:T(8,128)})) %all-reduce.15.cloned.1.call-update) | async-done | bytes 81936 | tf_op jit(solution)/shard_map/psum | solution.py:78
  (75 shorter events, 55.0 us)
Async XLA Ops:
  7.2 197.9 %all-reduce.21.cloned.1.call-start = ((), (), s32[]{:S(2)}) async-start(), calls=%async_computation.3 | async-start | bytes 262144 | tf_op jit(solution)/shard_map/psum | solution.py:78
  77.2 5.4 copy-start.11
  94.6 2.0 copy-start
  94.6 6.2 copy-start.4
  94.6 6.2 copy-start.10
  105.5 408.0 %all-reduce.19.cloned.1.call-start = ((), (), s32[]{:S(2)}) async-start(), calls=%async_computation.2 | async-start | bytes 262144 | tf_op jit(solution)/shard_map/psum | solution.py:78
  206.6 9.0 copy-start.5
  373.6 9.1 copy-start.6
  382.6 4.2 copy-start.13
  382.6 4.2 copy-start.2
  407.8 244.0 %all-reduce.17.cloned.1.call-start = ((), (), s32[]{:S(2)}) async-start(), calls=%async_computation.1 | async-start | bytes 262144 | tf_op jit(solution)/shard_map/psum | solution.py:78
  514.4 9.1 copy-start.7
  523.5 4.2 copy-start.14
  523.5 4.2 copy-start.3
  549.6 410.5 %all-reduce.15.cloned.1.call-start = ((), (), s32[]{:S(2)}) async-start(), calls=%async_computation | async-start | bytes 262144 | tf_op jit(solution)/shard_map/psum | solution.py:78
  652.7 9.0 copy-start.8
  820.2 9.1 copy-start.9
  829.2 4.2 copy-start.12
  829.2 4.2 copy-start.1
Sparse Core Ops, SparseCore 0:
  105.6 99.4 all-reduce.20
  407.9 105.5 all-reduce.18
  549.7 102.0 all-reduce.16
  854.5 105.5 all-reduce.14
